TPU v7x, 32 devices: a whole 2x2x4 slice. The times are simulated.
32 devices in a mesh: seq: 16 (over z, x, core), mlp: 2 (over y).
Axes of the slice: x: 2, y: 2, z: 4, core: 2. Of those that a mesh axis runs over, the one named last changes fastest.
Arguments:
- patches: bfloat16 [16384, 768], P(('seq', 'mlp')), may hold values from -6 to 6
- segments: int32 [16384], P(('seq', 'mlp')), may hold values from 0 to 5, as said below
- prompt_slots: int32 [16384], P(('seq', 'mlp')), may hold values from 0 to 50, as said below
- norm_gains: float32 [2, 2, 768], replicated, may hold values from 0.25 to 1.75
- qkv_weight: bfloat16 [2, 768, 2304], P(None, 'seq'), may hold values from -0.21875 to 0.21875
- out_weight: bfloat16 [2, 768, 768], P(None, 'seq'), may hold values from -0.875 to 0.875
- up_weight: bfloat16 [2, 768, 3072], P(None, 'seq', 'mlp'), may hold values from -0.21875 to 0.21875
- down_weight: bfloat16 [2, 3072, 768], P(None, 'mlp', 'seq'), may hold values from -0.15625 to 0.15625
- cotangent: bfloat16 [16384, 768], P(('seq', 'mlp')), may hold values from -6 to 6
- prompts: float32 [76800], P(('seq', 'mlp')), may hold values from -5 to 5
- first_moment: float32 [76800], P(('seq', 'mlp')), may hold values from -0.24 to 0.24
- second_moment: float32 [76800], P(('seq', 'mlp')), may hold values from 1e-05 to 0.015
- adam_betas: float32 [2], replicated, may hold values from 0.4 to 0.6
- learn_rate: float32 [1], replicated, may hold values from 0.2 to 0.6
Outputs:
- block_output: bfloat16 [16384, 768], P(('seq', 'mlp'))
- input_grad: float32 [16384, 768], P(('seq', 'mlp'))
- new_prompts: float32 [76800], P(('seq', 'mlp'))
- new_first: float32 [76800], P(('seq', 'mlp'))
- new_second: float32 [76800], P(('seq', 'mlp'))
- grad_norm: float32 [1], replicated
Inputs may be any that keep to these rules, and one draw needn't show every extreme that they name: `segments`: the 512 tokens of one device form aligned blocks in which whole images lie one after another, numbered 0, 1, 2 and so on; each image has 51 to 247 tokens, and every block holds an image of exactly 247 tokens. `prompt_slots`: the first 50 tokens of each image hold slots 0 to 49 in order; all other tokens hold 50.
All inputs are finite; a program needn't handle non-finite values.
Results may differ from a plain program's by a relative error of at most 0.02.
Values may be sent and summed in bfloat16 or wider, within the bound.
No kernel may reach another device: no remote copies, remote signals or barrier semaphores. Data moves between devices by JAX's collectives and lax.ppermute only.
A program may use at most 192 MiB of HBM per device.

v0:
```python
from functools import partial
import math
import jax
import jax.numpy as jnp
from jax import lax
from jax.sharding import PartitionSpec as P

HEADS = 12
HEAD_DIM = 64
ADAM_STEP = 2
ln_eps = 1e-06
masked_score = -1e30
clip_ratio = 0.05
adam_eps = 1e-08
decay_rate = 0.1
highest = lax.Precision.HIGHEST


def layer_norm(values, gain_row):
    center = values - jnp.mean(values, axis=-1, keepdims=True)
    spread = jnp.mean(center * center, axis=-1, keepdims=True)
    return center * lax.rsqrt(spread + ln_eps) * gain_row


def exact_gelu(values):
    return jax.nn.gelu(values, approximate=False)


def rows_times(piece_rows, weight):
    return jnp.dot(piece_rows, weight, preferred_element_type=jnp.float32)


def rows_times_back(piece_rows, weight):
    return jnp.einsum("td,fd->tf", piece_rows, weight, preferred_element_type=jnp.float32)


def slice_times(source, weight):
    return jnp.dot(source, weight, preferred_element_type=jnp.float32)


def slice_times_back(source, weight):
    return jnp.einsum("tf,df->td", source, weight, preferred_element_type=jnp.float32)


def masked_scores(query_rows, key_heads, seg_query, segments, score_scale):
    raw_scores = (
        jnp.einsum("qhd,khd->hqk", query_rows, key_heads, preferred_element_type=jnp.float32)
        * score_scale
    )
    allowed = (seg_query[:, None] == segments[None, :])[None]
    return jnp.where(allowed, raw_scores, masked_score)


def attend_forward(query_heads, key_heads, value_heads, segments, score_scale):
    tokens, head_count, head_depth = query_heads.shape
    block_rows = min(512, tokens)
    blocks = tokens // block_rows
    query_blocks = query_heads.reshape(blocks, block_rows, head_count, head_depth)
    seg_blocks = segments.reshape(blocks, block_rows)

    def one_block(block_pair):
        query_rows, seg_query = block_pair
        scores = masked_scores(query_rows, key_heads, seg_query, segments, score_scale)
        row_max = jnp.max(scores, axis=2, keepdims=True)
        exponent = jnp.exp(scores - row_max)
        row_total = jnp.sum(exponent, axis=2, keepdims=True)
        attn_probs = (exponent / row_total).astype(jnp.bfloat16)
        mixed_heads = jnp.einsum(
            "hqk,khd->qhd", attn_probs, value_heads, preferred_element_type=jnp.float32
        )
        return (mixed_heads.astype(jnp.bfloat16), row_max + jnp.log(row_total))

    mixed_heads, block_lse = lax.map(one_block, (query_blocks, seg_blocks))
    return (mixed_heads.reshape(tokens, head_count * head_depth), block_lse)


def attend_backward(
    query_heads, key_heads, value_heads, segments, block_lse, grad_mixed, score_scale
):
    tokens, head_count, head_depth = query_heads.shape
    block_rows = min(512, tokens)
    blocks = tokens // block_rows
    query_blocks = query_heads.reshape(blocks, block_rows, head_count, head_depth)
    grad_blocks = grad_mixed.reshape(blocks, block_rows, head_count, head_depth)
    seg_blocks = segments.reshape(blocks, block_rows)

    def one_block(running, block_parts):
        grad_keys, grad_values = running
        query_rows, grad_rows, seg_query, row_lse = block_parts
        scores = masked_scores(query_rows, key_heads, seg_query, segments, score_scale)
        attn_probs = jnp.exp(scores - row_lse)
        grad_probs = jnp.einsum(
            "qhd,khd->hqk", grad_rows, value_heads, preferred_element_type=jnp.float32
        )
        inner_sum = jnp.sum(attn_probs * grad_probs, axis=2, keepdims=True)
        grad_scores = (attn_probs * (grad_probs - inner_sum)).astype(jnp.bfloat16)
        grad_query = (
            jnp.einsum("hqk,khd->qhd", grad_scores, key_heads, preferred_element_type=jnp.float32)
            * score_scale
        )
        grad_keys = (
            grad_keys
            + jnp.einsum(
                "hqk,qhd->khd", grad_scores, query_rows, preferred_element_type=jnp.float32
            )
            * score_scale
        )
        grad_values = grad_values + jnp.einsum(
            "hqk,qhd->khd",
            attn_probs.astype(jnp.bfloat16),
            grad_rows,
            preferred_element_type=jnp.float32,
        )
        return ((grad_keys, grad_values), grad_query)

    zero_grads = jnp.zeros((tokens, head_count, head_depth), jnp.float32)
    (grad_keys, grad_values), grad_query = lax.scan(
        one_block, (zero_grads, zero_grads), (query_blocks, grad_blocks, seg_blocks, block_lse)
    )
    return (
        grad_query.reshape(tokens, head_count * head_depth),
        grad_keys.reshape(tokens, -1),
        grad_values.reshape(tokens, -1),
    )


def per_device(
    patches,
    segments,
    prompt_slots,
    norm_gains,
    qkv_weight,
    out_weight,
    up_weight,
    down_weight,
    cotangent,
    prompts,
    first_moment,
    second_moment,
    adam_betas,
    learn_rate,
):
    layers = norm_gains.shape[0]
    feature_width = norm_gains.shape[2]
    tokens = patches.shape[0]
    score_scale = HEAD_DIM ** (-0.5)
    gathered = lax.all_gather(prompts, ("seq", "mlp"), axis=0, tiled=True)
    prompt_table = gathered.reshape(layers, -1, feature_width)
    slot_total = prompt_table.shape[1]
    w_qkv, w_out, w_up, w_down = (
        lax.all_gather(qkv_weight, "seq", axis=1, tiled=True),
        lax.all_gather(out_weight, "seq", axis=1, tiled=True),
        lax.all_gather(up_weight, "seq", axis=1, tiled=True),
        lax.all_gather(down_weight, "seq", axis=2, tiled=True),
    )
    onehot = (prompt_slots[:, None] == jnp.arange(slot_total)[None, :]).astype(jnp.float32)
    is_prompt = (prompt_slots < slot_total)[:, None]
    hidden = patches.astype(jnp.float32)
    kept_state = []
    for layer_at in range(layers):
        inject = jnp.dot(onehot, prompt_table[layer_at], precision=highest)
        entry_rows = jnp.where(is_prompt, inject, hidden)
        normed_one, norm_one_back = jax.vjp(
            partial(layer_norm, gain_row=norm_gains[layer_at, 0]), entry_rows
        )
        qkv_proj = jnp.dot(
            normed_one.astype(jnp.bfloat16), w_qkv[layer_at], preferred_element_type=jnp.float32
        ).astype(jnp.bfloat16)
        query_heads = qkv_proj[:, :feature_width].reshape(tokens, HEADS, HEAD_DIM)
        key_heads = qkv_proj[:, feature_width : 2 * feature_width].reshape(tokens, HEADS, HEAD_DIM)
        value_heads = qkv_proj[:, 2 * feature_width :].reshape(tokens, HEADS, HEAD_DIM)
        mixed_rows, block_lse = attend_forward(
            query_heads, key_heads, value_heads, segments, score_scale
        )
        middle = entry_rows + jnp.dot(
            mixed_rows, w_out[layer_at], preferred_element_type=jnp.float32
        )
        normed_two, norm_two_back = jax.vjp(
            partial(layer_norm, gain_row=norm_gains[layer_at, 1]), middle
        )
        normed_low = normed_two.astype(jnp.bfloat16)
        before = rows_times(
            lax.all_gather(normed_low, "mlp", axis=0, tiled=True), weight=w_up[layer_at]
        )
        active = exact_gelu(before).astype(jnp.bfloat16)
        branch_two = lax.psum_scatter(
            slice_times(source=active, weight=w_down[layer_at]).astype(jnp.bfloat16),
            "mlp",
            scatter_dimension=0,
            tiled=True,
        ).astype(jnp.float32)
        hidden = middle + branch_two
        kept_state.append(
            (query_heads, key_heads, value_heads, block_lse, norm_one_back, norm_two_back, before)
        )
    block_output = hidden.astype(jnp.bfloat16)
    gradient = cotangent.astype(jnp.float32)
    layer_grads = []
    for layer_at in reversed(range(layers)):
        query_heads, key_heads, value_heads, block_lse, norm_one_back, norm_two_back, before = (
            kept_state[layer_at]
        )
        grad_low = gradient.astype(jnp.bfloat16)
        grad_active = rows_times_back(
            lax.all_gather(grad_low, "mlp", axis=0, tiled=True), weight=w_down[layer_at]
        )
        gelu_back = jax.vjp(exact_gelu, before)[1]
        grad_before = gelu_back(grad_active)[0].astype(jnp.bfloat16)
        grad_normtwo = lax.psum_scatter(
            slice_times_back(source=grad_before, weight=w_up[layer_at]).astype(jnp.bfloat16),
            "mlp",
            scatter_dimension=0,
            tiled=True,
        ).astype(jnp.float32)
        grad_middle = gradient + norm_two_back(grad_normtwo)[0]
        grad_branch = grad_middle.astype(jnp.bfloat16)
        grad_mixed = jnp.einsum(
            "te,de->td", grad_branch, w_out[layer_at], preferred_element_type=jnp.float32
        ).astype(jnp.bfloat16)
        grad_query, grad_keys, grad_values = attend_backward(
            query_heads,
            key_heads,
            value_heads,
            segments,
            block_lse,
            grad_mixed.reshape(tokens, HEADS, HEAD_DIM),
            score_scale,
        )
        grad_qkv = jnp.concatenate([grad_query, grad_keys, grad_values], axis=1).astype(
            jnp.bfloat16
        )
        grad_normone = jnp.einsum(
            "tc,dc->td", grad_qkv, w_qkv[layer_at], preferred_element_type=jnp.float32
        )
        grad_entry = grad_middle + norm_one_back(grad_normone)[0]
        layer_grads.append(jnp.einsum("tp,td->pd", onehot, grad_entry, precision=highest))
        gradient = jnp.where(is_prompt, 0.0, grad_entry)
    local_grads = jnp.stack(layer_grads[::-1]).reshape(-1)
    own_grads = lax.psum_scatter(local_grads, ("seq", "mlp"), scatter_dimension=0, tiled=True)
    square_sum = lax.psum(jnp.sum(own_grads * own_grads), ("seq", "mlp"))
    grad_norm = jnp.sqrt(square_sum)
    clip_limit = clip_ratio * math.sqrt(local_grads.shape[0])
    clipped = own_grads * jnp.minimum(1.0, clip_limit / (grad_norm + 1e-06))
    beta_one = adam_betas[0]
    beta_two = adam_betas[1]
    step_value = float(ADAM_STEP)
    new_first = beta_one * first_moment + (1.0 - beta_one) * clipped
    new_second = beta_two * second_moment + (1.0 - beta_two) * clipped * clipped
    first_hat = new_first / (1.0 - beta_one**step_value)
    second_hat = new_second / (1.0 - beta_two**step_value)
    new_prompts = prompts - learn_rate[0] * (
        first_hat / (jnp.sqrt(second_hat) + adam_eps) + decay_rate * prompts
    )
    return (block_output, gradient, new_prompts, new_first, new_second, grad_norm.reshape(1))


def solution(mesh):
    in_specs = (
        P(("seq", "mlp"), None),
        P(("seq", "mlp")),
        P(("seq", "mlp")),
        P(),
        P(None, "seq", None),
        P(None, "seq", None),
        P(None, "seq", "mlp"),
        P(None, "mlp", "seq"),
        P(("seq", "mlp"), None),
        P(("seq", "mlp")),
        P(("seq", "mlp")),
        P(("seq", "mlp")),
        P(),
        P(),
    )
    out_specs = (
        P(("seq", "mlp"), None),
        P(("seq", "mlp"), None),
        P(("seq", "mlp")),
        P(("seq", "mlp")),
        P(("seq", "mlp")),
        P(),
    )
    return jax.shard_map(
        per_device, mesh=mesh, in_specs=in_specs, out_specs=out_specs, check_vma=False
    )
```

profile of v0, /device:TPU:0, one launch (start us, length us, event | category | flops | bytes accessed | tf_op | source)
XLA Modules:
  0.0 815.6 jit_solution(11228677048224738187)
XLA Ops:
  14.0 175.3 %all-reduce.5.cloned.1.call-done = f32[76800]{0:T(1024)} async-done(((f32[76800]{0:T(1024)}), f32[76800]{0:T(1024)}) %all-reduce.5.cloned.1.call-update) | async-done | bytes 307216
  189.4 1.7 fusion.104
  191.1 2.1 fusion.106
  193.6 4.3 convolution_convert_fusion.1
  197.9 1.3 fusion.103
  199.5 1.7 copy.61
  201.2 2.6 copy.60
  203.8 2.1 fusion.24
  205.9 2.6 fusion
  208.5 1.9 copy-done
  210.4 4.8 fusion.59
  215.2 2.4 fusion.107
  218.2 1.1 multiply_convert_fusion.16
  220.2 26.3 %all-gather.13.cloned.1.call-done = bf16[1024,768]{1,0:T(8,128)(2,1)} async-done(((bf16[512,768]{1,0:T(8,128)(2,1)}), bf16[1024,768]{1,0:T(8,128)(2,1)}) %all-gather.13.cloned.1.call-update) | async-done | bytes 1572880 | tf_op jit(solution)/shard_map/all_gather | solution.py:183
  246.6 19.2 %fusion.4 = (f32[1024,1536]{1,0:T(8,128)}, f32[1024,1536]{1,0:T(8,128)}) fusion(bf16[1024,768]{1,0:T(8,128)(2,1)} %all-gather.13.cloned.1.call-done, bf16[2,768,1536]{2,1,0:T(8,128)(2,1)} %all-gather.15.cloned.1.call-done), kind=kOutput, calls=%fused_computation.18 | convolution fusion | flops 2513436672 | bytes 16515072 | tf_op jit(solution)/shard_map/dot_general | solution.py:30
  265.8 36.5 %all-gather.17.cloned.1.call-done = bf16[2,1536,768]{1,2,0:T(8,128)(2,1)} async-done(((bf16[2,1536,48]{1,2,0:T(8,128)(2,1)}), bf16[2,1536,768]{1,2,0:T(8,128)(2,1)}) %all-gather.17.cloned.1.call-update) | async-done | bytes 4718608 | tf_op jit(solution)/shard_map/all_gather | solution.py:154
  302.3 9.1 %fusion.51 = bf16[1024,768]{1,0:T(8,128)(2,1)} fusion(bf16[2,1536,768]{1,2,0:T(8,128)(2,1)} %all-gather.17.cloned.1.call-done, f32[1024,1536]{1,0:T(8,128)} %get-tuple-element.152, f32[1024,1536]{1,0:T(8,128)} %get-tuple-element.153), kind=kOutput, calls=%fused_computation.95 | convolution fusion | flops 2421424128 | bytes 16515072 | tf_op jit(solution)/shard_map/dot_general | solution.py:38
  311.7 24.4 %reduce-scatter.5.cloned.1.call-done = bf16[512,768]{1,0:T(8,128)(2,1)} async-done(((bf16[1024,768]{1,0:T(8,128)(2,1)}), bf16[512,768]{1,0:T(8,128)(2,1)}) %reduce-scatter.5.cloned.1.call-update) | async-done | bytes 786448 | tf_op jit(solution)/shard_map/reduce_scatter | solution.py:186
  336.0 2.1 fusion.108
  338.5 4.3 convolution_convert_fusion
  342.8 1.3 fusion.102
  344.4 1.7 copy.65
  346.2 2.6 copy.64
  348.7 2.1 fusion.25
  350.9 2.6 fusion.1
  353.4 1.9 copy-done.1
  355.4 3.6 fusion.58
  360.2 1.2 multiply_convert_fusion.14
  362.2 26.3 %all-gather.19.cloned.1.call-done = bf16[1024,768]{1,0:T(8,128)(2,1)} async-done(((bf16[512,768]{1,0:T(8,128)(2,1)}), bf16[1024,768]{1,0:T(8,128)(2,1)}) %all-gather.19.cloned.1.call-update) | async-done | bytes 1572880 | tf_op jit(solution)/shard_map/all_gather | solution.py:183
  388.6 18.9 %fusion.5 = (f32[1024,1536]{1,0:T(8,128)}, f32[1024,1536]{1,0:T(8,128)}) fusion(bf16[1024,768]{1,0:T(8,128)(2,1)} %all-gather.19.cloned.1.call-done, bf16[2,768,1536]{2,1,0:T(8,128)(2,1)} %all-gather.15.cloned.1.call-done), kind=kOutput, calls=%fused_computation.19 | convolution fusion | flops 2513436672 | bytes 16515072 | tf_op jit(solution)/shard_map/dot_general | solution.py:30
  407.4 9.7 %all-gather.21.cloned.1.call-done = bf16[1024,768]{1,0:T(8,128)(2,1)} async-done(((bf16[512,768]{1,0:T(8,128)(2,1)}), bf16[1024,768]{1,0:T(8,128)(2,1)}) %all-gather.21.cloned.1.call-update) | async-done | bytes 1572880 | tf_op jit(solution)/shard_map/all_gather | solution.py:205
  417.1 13.0 %fusion.49 = bf16[1024,768]{1,0:T(8,128)(2,1)} fusion(bf16[2,768,1536]{2,1,0:T(8,128)(2,1)} %all-gather.15.cloned.1.call-done, f32[1024,1536]{1,0:T(8,128)} %get-tuple-element.160, f32[1024,1536]{1,0:T(8,128)} %get-tuple-element.161, bf16[1024,768]{1,0:T(8,128)(2,1)} %all-gather.21.cloned.1.call-done, bf16[2,1536,768]{1,2,0:T(8,128)(2,1)} %all-gather.17.cloned.1.call-done), kind=kOutput, calls=%fused_computation.93 | convolution fusion | flops 4854644736 | bytes 20447232 | tf_op jit(solution)/shard_map/tf,df->td/dot_general | solution.py:42
  430.1 9.1 %fusion.50 = bf16[1024,768]{1,0:T(8,128)(2,1)} fusion(bf16[2,1536,768]{1,2,0:T(8,128)(2,1)} %all-gather.17.cloned.1.call-done, f32[1024,1536]{1,0:T(8,128)} %get-tuple-element.160, f32[1024,1536]{1,0:T(8,128)} %get-tuple-element.161), kind=kOutput, calls=%fused_computation.94 | convolution fusion | flops 2421424128 | bytes 16515072 | tf_op jit(solution)/shard_map/dot_general | solution.py:38
  439.7 16.4 %reduce-scatter.9.cloned.1.call-done = bf16[512,768]{1,0:T(8,128)(2,1)} async-done(((bf16[1024,768]{1,0:T(8,128)(2,1)}), bf16[512,768]{1,0:T(8,128)(2,1)}) %reduce-scatter.9.cloned.1.call-update) | async-done | bytes 786448 | tf_op jit(solution)/shard_map/reduce_scatter | solution.py:209
  456.2 1.5 multiply_reduce_fusion.5
  457.7 26.8 %reduce-scatter.7.cloned.1.call-done = bf16[512,768]{1,0:T(8,128)(2,1)} async-done(((bf16[1024,768]{1,0:T(8,128)(2,1)}), bf16[512,768]{1,0:T(8,128)(2,1)}) %reduce-scatter.7.cloned.1.call-update) | async-done | bytes 786448 | tf_op jit(solution)/shard_map/reduce_scatter | solution.py:186
  484.5 2.9 fusion.101
  487.5 1.1 copy-done.17
  488.6 2.4 convolution_convert_fusion.3
  491.3 7.3 fusion.52
  498.7 9.6 %multiply_reduce_fusion.1 = (f32[12,512]{1,0:T(8,128)S(1)}, f32[12,512,512]{1,2,0:T(8,128)}) fusion(f32[12,512]{1,0:T(8,128)S(1)} %log_add_fusion.1, f32[12,512,512]{1,2,0:T(8,128)} %copy-done.1, pred[512,512]{0,1:T(8,128)(4,1)S(1)} %broadcast_compare_fusion, bf16[512,12,64]{0,2,1:T(8,128)(2,1)S(1)} %bitcast.151, bf16[512,12,64]{0,2,1:T(8,128)(2,1)S(1)} %bitcast.149), kind=kOutput, calls=%fused_computation.4 | convolution fusion | flops 418375680 | bytes 27049984 | tf_op jit(solution)/shard_map/while/body/eval_jaxpr/qhd,khd->hqk/dot_general | solution.py:92
  508.3 7.1 multiply_convert_fusion.1
  515.4 2.0 multiply_convert_fusion.12
  519.9 2.3 multiply_reduce_fusion.4
  522.9 1.4 select_convert_fusion
  524.6 26.9 %all-gather.23.cloned.1.call-done = bf16[1024,768]{1,0:T(8,128)(2,1)} async-done(((bf16[512,768]{1,0:T(8,128)(2,1)}), bf16[1024,768]{1,0:T(8,128)(2,1)}) %all-gather.23.cloned.1.call-update) | async-done | bytes 1572880 | tf_op jit(solution)/shard_map/all_gather | solution.py:205
  551.4 13.0 %fusion.48 = bf16[1024,768]{1,0:T(8,128)(2,1)} fusion(bf16[2,768,1536]{2,1,0:T(8,128)(2,1)} %all-gather.15.cloned.1.call-done, f32[1024,1536]{1,0:T(8,128)} %get-tuple-element.152, f32[1024,1536]{1,0:T(8,128)} %get-tuple-element.153, bf16[1024,768]{1,0:T(8,128)(2,1)} %all-gather.23.cloned.1.call-done, bf16[2,1536,768]{1,2,0:T(8,128)(2,1)} %all-gather.17.cloned.1.call-done), kind=kOutput, calls=%fused_computation.92 | convolution fusion | flops 4854644736 | bytes 20447232 | tf_op jit(solution)/shard_map/tf,df->td/dot_general | solution.py:42
  564.5 1.5 convolution_bitcast_fusion
  566.0 24.5 %reduce-scatter.11.cloned.1.call-done = bf16[512,768]{1,0:T(8,128)(2,1)} async-done(((bf16[1024,768]{1,0:T(8,128)(2,1)}), bf16[512,768]{1,0:T(8,128)(2,1)}) %reduce-scatter.11.cloned.1.call-update) | async-done | bytes 786448 | tf_op jit(solution)/shard_map/reduce_scatter | solution.py:209
  590.5 1.7 multiply_reduce_fusion.3
  592.2 1.8 fusion.97
  594.0 2.2 add_add_fusion.5
  597.4 7.5 fusion.55
  604.9 9.5 %multiply_reduce_fusion = (f32[12,512]{1,0:T(8,128)S(1)}, f32[12,512,512]{1,2,0:T(8,128)}) fusion(f32[12,512]{1,0:T(8,128)S(1)} %log_add_fusion, f32[12,512,512]{1,2,0:T(8,128)} %copy-done, pred[512,512]{0,1:T(8,128)(4,1)S(1)} %broadcast_compare_fusion, bf16[512,12,64]{0,2,1:T(8,128)(2,1)S(1)} %bitcast.153, bf16[512,12,64]{0,2,1:T(8,128)(2,1)S(1)} %bitcast.147), kind=kOutput, calls=%fused_computation.1 | convolution fusion | flops 418375680 | bytes 27049984 | tf_op jit(solution)/shard_map/while/body/eval_jaxpr/qhd,khd->hqk/dot_general | solution.py:92
  614.5 7.1 multiply_convert_fusion
  621.6 2.0 multiply_convert_fusion.10
  623.6 1.1 multiply_convert_fusion.11
  626.1 2.2 multiply_reduce_fusion.2
  629.1 1.1 copy-done.7
  637.0 120.7 %all-reduce.7.cloned.1.call-done = f32[76800]{0:T(1024)} async-done(((f32[76800]{0:T(1024)}), f32[76800]{0:T(1024)}) %all-reduce.7.cloned.1.call-update) | async-done | bytes 307216
  757.8 1.4 multiply_reduce_fusion.10
  759.2 2.8 broadcast_select_fusion
  762.0 41.4 %psum.7 = f32[]{:T(128)} all-reduce(f32[]{:T(128)} %multiply_reduce_fusion.10), channel_id=1, replica_groups=mesh['seq'=16,'mlp'=2] {'seq','mlp'}, use_global_device_ids=true, to_apply=%region_28.29 | all-reduce | flops 1 | bytes 8 | tf_op jit(solution)/shard_map/psum | solution.py:240
  804.1 2.7 multiply_subtract_fusion
  (205 shorter events, 20.8 us)
Async XLA Ops:
  8.0 181.4 %all-reduce.5.cloned.1.call-start = ((), (), s32[]{:S(2)}) async-start(), calls=%async_computation.16 | async-start | bytes 614400
  9.7 183.8 %all-gather.9.cloned.1.call-start = ((), (), s32[]{:S(2)}) async-start(), calls=%async_computation.4 | async-start | bytes 7520256 | tf_op jit(solution)/shard_map/all_gather | solution.py:151
  10.3 204.9 %all-gather.11.cloned.1.call-start = ((), (), s32[]{:S(2)}) async-start(), calls=%async_computation.5 | async-start | bytes 2506752 | tf_op jit(solution)/shard_map/all_gather | solution.py:152
  10.9 209.3 %all-gather.15.cloned.1.call-start = ((), (), s32[]{:S(2)}) async-start(), calls=%async_computation.7 | async-start | bytes 5013504 | tf_op jit(solution)/shard_map/all_gather | solution.py:153
  11.5 235.1 %all-gather.13.cloned.1.call-start = ((), (), s32[]{:S(2)}) async-start(), calls=%async_computation.6 | async-start | bytes 2359296 | tf_op jit(solution)/shard_map/all_gather | solution.py:183
  12.4 185.5 %copy-start.47 = (f32[768]{0:T(1024)}, f32[768]{0:T(1024)S(1)}, u32[]{:S(2)}) copy-start(f32[768]{0:T(1024)S(1)} %get-tuple-element.89) | copy-start | bytes 9220
  12.4 205.6 %copy-start.33 = (f32[768]{0:T(1024)}, f32[768]{0:T(1024)S(1)}, u32[]{:S(2)}) copy-start(f32[768]{0:T(1024)S(1)} %get-tuple-element.88) | copy-start | bytes 9220
  193.2 22.0 %copy-start.5 = (f32[512,768]{1,0:T(8,128)}, f32[512,768]{1,0:T(8,128)S(1)}, u32[]{:S(2)}) copy-start(f32[512,768]{1,0:T(8,128)S(1)} %get-tuple-element.136) | copy-start | bytes 4718596
  193.2 4.7 copy-start.41
  193.5 5.7 copy-start.43
  193.6 5.6 copy-start.51
  199.5 6.4 copy-start.9
  201.2 4.7 copy-start.13
  205.9 4.5 copy-start
  205.9 4.5 copy-start.29
  205.9 4.5 copy-start.19
  218.0 47.8 %copy-start.45 = (f32[512]{0:T(512)}, f32[512]{0:T(512)S(1)}, u32[]{:S(2)}) copy-start(f32[512]{0:T(512)S(1)} %multiply_reduce_fusion.8) | copy-start | bytes 6148
  218.0 47.8 %copy-start.39 = (f32[512]{0:T(512)}, f32[512]{0:T(512)S(1)}, u32[]{:S(2)}) copy-start(f32[512]{0:T(512)S(1)} %fusion.76) | copy-start | bytes 6148
  219.4 82.9 %all-gather.17.cloned.1.call-start = ((), (), s32[]{:S(2)}) async-start(), calls=%async_computation.8 | async-start | bytes 5013504 | tf_op jit(solution)/shard_map/all_gather | solution.py:154
  220.2 115.9 %reduce-scatter.5.cloned.1.call-start = ((), (), s32[]{:S(2)}) async-start(), calls=%async_computation.9 | async-start | bytes 2359296 | tf_op jit(solution)/shard_map/reduce_scatter | solution.py:186
  302.3 9.3 %copy-start.28 = (f32[38400]{0:T(1024)S(1)}, f32[38400]{0:T(1024)}, u32[]{:S(2)}) copy-start(f32[38400]{0:T(1024)} %get-tuple-element.131) | copy-start | bytes 460804
  302.3 33.8 %copy-start.37 = (s32[512]{0:T(512)S(1)}, s32[512]{0:T(512)}, u32[]{:S(2)}) copy-start(s32[512]{0:T(512)} %param.16) | copy-start | bytes 6148
  311.4 77.2 %all-gather.19.cloned.1.call-start = ((), (), s32[]{:S(2)}) async-start(), calls=%async_computation.10 | async-start | bytes 2359296 | tf_op jit(solution)/shard_map/all_gather | solution.py:183
  338.2 4.7 copy-start.2
  344.4 6.4 copy-start.11
  346.1 4.7 copy-start.15
  350.8 4.5 copy-start.1
  350.8 4.5 copy-start.21
  355.4 3.6 copy-start.3
  355.4 3.6 copy-start.24
  361.4 55.7 %all-gather.21.cloned.1.call-start = ((), (), s32[]{:S(2)}) async-start(), calls=%async_computation.12 | async-start | bytes 2359296 | tf_op jit(solution)/shard_map/all_gather | solution.py:205
  362.0 94.2 %reduce-scatter.9.cloned.1.call-start = ((), (), s32[]{:S(2)}) async-start(), calls=%async_computation.13 | async-start | bytes 2359296 | tf_op jit(solution)/shard_map/reduce_scatter | solution.py:209
  430.1 54.4 %reduce-scatter.7.cloned.1.call-start = ((), (), s32[]{:S(2)}) async-start(), calls=%async_computation.11 | async-start | bytes 2359296 | tf_op jit(solution)/shard_map/reduce_scatter | solution.py:186
  439.3 112.2 %all-gather.23.cloned.1.call-start = ((), (), s32[]{:S(2)}) async-start(), calls=%async_computation.14 | async-start | bytes 2359296 | tf_op jit(solution)/shard_map/all_gather | solution.py:205
  491.3 7.4 copy-start.22
  491.3 17.0 %slice-start.3 = ((s8[12582912]{0:T(1024)(128)(4,1)}), s8[4194304]{0:T(1024)(128)(4,1)S(1)}, s32[]{:S(2)}) async-start(s8[12582912]{0:T(1024)(128)(4,1)} %bitcast.136), calls=%async_computation.21 | async-start | bytes 8388608
  491.3 17.0 %slice-start.4 = ((s8[12582912]{0:T(1024)(128)(4,1)}), s8[4194304]{0:T(1024)(128)(4,1)S(1)}, s32[]{:S(2)}) async-start(s8[12582912]{0:T(1024)(128)(4,1)} %bitcast.136), calls=%async_computation.22 | async-start | bytes 8388608
  498.7 9.6 %slice-start.5 = ((s8[12582912]{0:T(1024)(128)(4,1)}), s8[4194304]{0:T(1024)(128)(4,1)S(1)}, s32[]{:S(2)}) async-start(s8[12582912]{0:T(1024)(128)(4,1)} %bitcast.136), calls=%async_computation.23 | async-start | bytes 8388608
  508.3 7.1 copy-start.16
  515.4 3.2 slice-start.6
  517.5 2.5 copy-start.55
  519.9 2.9 copy-start.18
  519.9 2.9 copy-start.23
  524.3 40.3 %copy-start.8 = (f32[512,768]{1,0:T(8,128)}, f32[512,768]{1,0:T(8,128)S(1)}, u32[]{:S(2)}) copy-start(f32[512,768]{1,0:T(8,128)S(1)} %get-tuple-element.108) | copy-start | bytes 4718596
  524.3 40.2 %copy-start.30 = (f32[12,512]{1,0:T(8,128)S(1)}, f32[12,512]{1,0:T(8,128)}, u32[]{:S(2)}) copy-start(f32[12,512]{1,0:T(8,128)} %copy-done.29) | copy-start | bytes 73732
  524.3 40.2 %copy-start.32 = (f32[12,512]{1,0:T(8,128)S(1)}, f32[12,512]{1,0:T(8,128)}, u32[]{:S(2)}) copy-start(f32[12,512]{1,0:T(8,128)} %copy-done.31) | copy-start | bytes 73732
  524.3 66.2 %copy-start.34 = (f32[768]{0:T(1024)S(1)}, f32[768]{0:T(1024)}, u32[]{:S(2)}) copy-start(f32[768]{0:T(1024)} %copy-done.33) | copy-start | bytes 9220
  524.3 66.2 %copy-start.36 = (f32[512]{0:T(512)S(1)}, f32[512]{0:T(512)}, u32[]{:S(2)}) copy-start(f32[512]{0:T(512)} %copy-done.35) | copy-start | bytes 6148
  524.3 67.9 %copy-start.46 = (f32[512]{0:T(512)S(1)}, f32[512]{0:T(512)}, u32[]{:S(2)}) copy-start(f32[512]{0:T(512)} %copy-done.45) | copy-start | bytes 6148
  524.3 67.9 %copy-start.40 = (f32[512]{0:T(512)S(1)}, f32[512]{0:T(512)}, u32[]{:S(2)}) copy-start(f32[512]{0:T(512)} %copy-done.39) | copy-start | bytes 6148
  524.3 66.2 %reduce-scatter.11.cloned.1.call-start = ((), (), s32[]{:S(2)}) async-start(), calls=%async_computation.15 | async-start | bytes 2359296 | tf_op jit(solution)/shard_map/reduce_scatter | solution.py:209
  564.4 193.3 %all-reduce.7.cloned.1.call-start = ((), (), s32[]{:S(2)}) async-start(), calls=%async_computation.17 | async-start | bytes 614400
  590.5 5.7 copy-start.25
  597.4 7.6 copy-start.20
  597.4 17.1 %slice-start = ((s8[12582912]{0:T(1024)(128)(4,1)}), s8[4194304]{0:T(1024)(128)(4,1)S(1)}, s32[]{:S(2)}) async-start(s8[12582912]{0:T(1024)(128)(4,1)} %bitcast.134), calls=%async_computation.18 | async-start | bytes 8388608
  597.4 17.1 %slice-start.1 = ((s8[12582912]{0:T(1024)(128)(4,1)}), s8[4194304]{0:T(1024)(128)(4,1)S(1)}, s32[]{:S(2)}) async-start(s8[12582912]{0:T(1024)(128)(4,1)} %bitcast.134), calls=%async_computation.19 | async-start | bytes 8388608
  604.9 9.5 %slice-start.2 = ((s8[12582912]{0:T(1024)(128)(4,1)}), s8[4194304]{0:T(1024)(128)(4,1)S(1)}, s32[]{:S(2)}) async-start(s8[12582912]{0:T(1024)(128)(4,1)} %bitcast.134), calls=%async_computation.20 | async-start | bytes 8388608
  614.5 7.1 copy-start.14
  621.6 3.2 slice-start.8
  628.4 2.8 copy-start.27
  628.4 3.6 copy-start.53
  628.4 175.7 %copy-start.38 = (f32[2400]{0:T(1024)S(1)}, f32[2400]{0:T(1024)}, u32[]{:S(2)}) copy-start(f32[2400]{0:T(1024)} %param.23) | copy-start | bytes 28804
  628.4 175.7 %copy-start.49 = (f32[2400]{0:T(1024)S(1)}, f32[2400]{0:T(1024)}, u32[]{:S(2)}) copy-start(f32[2400]{0:T(1024)} %param.25) | copy-start | bytes 28804
  628.4 175.7 %copy-start.50 = (f32[2400]{0:T(1024)S(1)}, f32[2400]{0:T(1024)}, u32[]{:S(2)}) copy-start(f32[2400]{0:T(1024)} %param.24) | copy-start | bytes 28804
  (16 other events, 27.4 us)
Sparse Core Ops, SparseCore 0:
  14.8 174.5 all-reduce.4
  632.1 125.6 all-reduce.6
Sparse Core Ops, SparseCore 1:
  12.5 69.7 all-gather.8
  84.4 41.0 all-gather.10
  127.6 52.1 all-gather.14
  219.5 27.0 all-gather.12
  249.1 53.1 all-gather.16
  311.5 24.5 reduce-scatter.4
  361.5 27.0 all-gather.18
  390.0 27.1 all-gather.20
  430.2 25.9 reduce-scatter.8
  458.5 25.9 reduce-scatter.6
  524.4 27.0 all-gather.22
  564.5 25.9 reduce-scatter.10
where the time goes:
time: 824 us; the launch traced here: 816 us
  waiting for transfers between devices  517 us (63%)
  matrix products  161 us (20%)
  other arithmetic  44.2 us (5%)
  blocking collectives  41.4 us (5%)
  local copies, waits for them, and re-layouts  27.1 us (3%)
  between operations  23.2 us (3%)
    unnamed x16, waiting for transfers between devices  299 us
    all_gather x2, waiting for transfers between devices, per_device(): lax.all_gather(normed_low, 'mlp', axis=0, tiled=True)  52.7 us
    reduce_scatter x2, waiting for transfers between devices, per_device(): lax.psum_scatter(slice_times(source=active, weight=w_down[layer_at]).asty...  51.2 us
    psum x1, blocking collectives, per_device(): square_sum = lax.psum(jnp.sum(own_grads * own_grads), ('seq', 'mlp'))  41.4 us
    reduce_scatter x2, waiting for transfers between devices, per_device(): lax.psum_scatter(slice_times_back(source=grad_before, weight=w_up[layer_a...  41 us
    dot_general x2, matrix products, rows_times(): return jnp.dot(piece_rows, weight, preferred_element_type=jnp.float32)  38.1 us
    all_gather x2, waiting for transfers between devices, per_device(): lax.all_gather(grad_low, 'mlp', axis=0, tiled=True)  36.5 us
    all_gather x1, waiting for transfers between devices, per_device(): lax.all_gather(down_weight, 'seq', axis=2, tiled=True)  36.5 us
  transfers between devices with their start and end apart: 14, of which 11 were waited for; matrix products, arithmetic and copies ran while one was open for 10% of the time, Pallas kernels for 0%

commit v1 on v0

--- a/solution.py
+++ b/solution.py
@@ -14,6 +14,28 @@
 adam_eps = 1e-08
 decay_rate = 0.1
 highest = lax.Precision.HIGHEST
+
+
+def joined_along(parts, dim):
+    parts = jnp.moveaxis(parts, 0, dim)
+    dims = parts.shape
+    return parts.reshape(*dims[:dim], dims[dim] * dims[dim + 1], *dims[dim + 2 :])
+
+
+def collected_by_bits(value, axis):
+    size = lax.axis_size(axis)
+    parts = value[None]
+    for level in range(size.bit_length() - 1):
+        apart = 1 << level
+        other = lax.ppermute(parts, axis, [(i, i ^ apart) for i in range(size)])
+        both = jnp.stack([parts, other])
+        upper = lax.axis_index(axis) >> level & 1
+        parts = jnp.where(upper == 0, both, both[::-1]).reshape(-1, *value.shape)
+    return parts
+
+
+def collect(shard, axis, dim):
+    return joined_along(collected_by_bits(shard, axis), dim)
 
 
 def layer_norm(values, gain_row):
@@ -179,9 +201,7 @@
             partial(layer_norm, gain_row=norm_gains[layer_at, 1]), middle
         )
         normed_low = normed_two.astype(jnp.bfloat16)
-        before = rows_times(
-            lax.all_gather(normed_low, "mlp", axis=0, tiled=True), weight=w_up[layer_at]
-        )
+        before = rows_times(collect(normed_low, "mlp", 0), weight=w_up[layer_at])
         active = exact_gelu(before).astype(jnp.bfloat16)
         branch_two = lax.psum_scatter(
             slice_times(source=active, weight=w_down[layer_at]).astype(jnp.bfloat16),

time: 824 us -> 773 us (0.938)
  waiting for transfers between devices: 517 us -> 465 us
    all_gather x2 -> x0, waiting for transfers between devices: 52.7 us -> none  [per_device(): lax.all_gather(normed_low, 'mlp', axis=0, tiled=True)]
    ppermute x0 -> x2, waiting for transfers between devices: none -> 43.9 us  [collected_by_bits(): other = lax.ppermute(parts, axis, [(i, i ^ apart) for i in range(size)])]
    all_gather x1, waiting for transfers between devices: 36.5 us -> 0.01 us  [per_device(): lax.all_gather(down_weight, 'seq', axis=2, tiled=True)]
    all_gather x2, waiting for transfers between devices: 36.5 us -> 27.1 us  [per_device(): lax.all_gather(grad_low, 'mlp', axis=0, tiled=True)]
    unnamed x16 -> x14, waiting for transfers between devices: 299 us -> 299 us
  transfers between devices with their start and end apart: 14 -> 14, of which waited for: 11 -> 9; matrix products, arithmetic and copies ran while one was open for 10% -> 11% of each run, Pallas kernels for 0% -> 0%
where the time goes in v1:
time: 773 us; the launch traced here: 765 us
  waiting for transfers between devices  465 us (60%)
  matrix products  162 us (21%)
  other arithmetic  44.4 us (6%)
  blocking collectives  41.4 us (5%)
  local copies, waits for them, and re-layouts  25.7 us (3%)
  between operations  23.4 us (3%)
    unnamed x14, waiting for transfers between devices  299 us
    reduce_scatter x2, waiting for transfers between devices, per_device(): lax.psum_scatter(slice_times(source=active, weight=w_down[layer_at]).asty...  53.4 us
    ppermute x2, waiting for transfers between devices, collected_by_bits(): other = lax.ppermute(parts, axis, [(i, i ^ apart) for i in range(size)])  43.9 us
    psum x1, blocking collectives, per_device(): square_sum = lax.psum(jnp.sum(own_grads * own_grads), ('seq', 'mlp'))  41.4 us
    reduce_scatter x2, waiting for transfers between devices, per_device(): lax.psum_scatter(slice_times_back(source=grad_before, weight=w_up[layer_a...  41.3 us
    dot_general x2, matrix products, rows_times(): return jnp.dot(piece_rows, weight, preferred_element_type=jnp.float32)  36.8 us
    all_gather x2, waiting for transfers between devices, per_device(): lax.all_gather(grad_low, 'mlp', axis=0, tiled=True)  27.1 us
    dot_general x2, matrix products, slice_times_back(): jnp.einsum('tf,df->td', source, weight, preferred_element_type=jnp.float32)  25.9 us
  transfers between devices with their start and end apart: 14, of which 9 were waited for; matrix products, arithmetic and copies ran while one was open for 11% of the time, Pallas kernels for 0%

profile of v1, /device:TPU:0, one launch (start us, length us, event | category | flops | bytes accessed | tf_op | source)
XLA Modules:
  0.0 764.6 jit_solution(17248771407965985237)
XLA Ops:
  8.1 0.9 dynamic-update-slice
  13.8 1.0 broadcast_compare_fusion
  14.8 175.8 %all-reduce.5.cloned.1.call-done = f32[76800]{0:T(1024)} async-done(((f32[76800]{0:T(1024)}), f32[76800]{0:T(1024)}) %all-reduce.5.cloned.1.call-update) | async-done | bytes 307216
  190.6 1.7 fusion.104
  192.3 2.1 fusion.106
  194.8 4.3 convolution_convert_fusion.1
  199.1 1.3 fusion.103
  200.7 1.7 copy.61
  202.4 2.1 fusion.24
  204.6 2.6 fusion
  207.1 2.1 copy-done
  209.5 8.0 %fusion.59 = bf16[12,64,512]{2,1,0:T(8,128)(2,1)} fusion(bf16[512,12,64]{0,2,1:T(8,128)(2,1)S(1)} %bitcast.158, f32[12,512]{1,0:T(8,128)S(1)} %fusion, f32[12,512]{1,0:T(8,128)S(1)} %get-tuple-element.137, f32[12,512,512]{1,2,0:T(8,128)} %copy-done, pred[512,512]{0,1:T(8,128)(4,1)S(1)} %broadcast_compare_fusion), kind=kOutput, calls=%fused_computation.133 | convolution fusion | flops 418775040 | bytes 14467072 | tf_op jit(solution)/shard_map/while/body/eval_jaxpr/hqk,khd->qhd/dot_general | solution.py:90
  217.5 2.4 fusion.107
  220.5 1.5 collective-permute-start
  222.3 16.5 %collective-permute-done = bf16[1,512,768]{2,1,0:T(8,128)(2,1)S(1)} collective-permute-done((bf16[1,512,768]{2,1,0:T(8,128)(2,1)S(1)}, bf16[1,512,768]{2,1,0:T(8,128)(2,1)S(1)}, u32[]{:S(2)}, u32[]{:S(2)}) %collective-permute-start) | collective-permute-done | bytes 786464 | tf_op jit(solution)/shard_map/ppermute | solution.py:30
  239.4 18.4 %fusion.4 = (f32[1024,1536]{1,0:T(8,128)}, f32[1024,1536]{1,0:T(8,128)}) fusion(bf16[1024,768]{1,0:T(8,128)(2,1)S(1)} %bitcast.168, bf16[2,768,1536]{2,1,0:T(8,128)(2,1)} %all-gather.11.cloned.1.call-done), kind=kOutput, calls=%fused_computation.18 | convolution fusion | flops 2513436672 | bytes 16515072 | tf_op jit(solution)/shard_map/dot_general | solution.py:52
  257.8 9.1 %fusion.51 = bf16[1024,768]{1,0:T(8,128)(2,1)} fusion(bf16[2,1536,768]{1,2,0:T(8,128)(2,1)} %all-gather.13.cloned.1.call-done, f32[1024,1536]{1,0:T(8,128)} %get-tuple-element.152, f32[1024,1536]{1,0:T(8,128)} %get-tuple-element.153), kind=kOutput, calls=%fused_computation.97 | convolution fusion | flops 2421424128 | bytes 16515072 | tf_op jit(solution)/shard_map/dot_general | solution.py:60
  267.2 26.7 %reduce-scatter.5.cloned.1.call-done = bf16[512,768]{1,0:T(8,128)(2,1)} async-done(((bf16[1024,768]{1,0:T(8,128)(2,1)}), bf16[512,768]{1,0:T(8,128)(2,1)}) %reduce-scatter.5.cloned.1.call-update) | async-done | bytes 786448 | tf_op jit(solution)/shard_map/reduce_scatter | solution.py:206
  293.9 2.1 fusion.108
  296.3 4.3 convolution_convert_fusion
  300.7 1.3 fusion.102
  302.3 1.7 copy.65
  304.0 2.6 copy.64
  306.6 2.1 fusion.25
  308.7 2.6 fusion.1
  311.2 1.9 copy-done.1
  313.2 3.6 fusion.58
  318.0 1.2 fusion.140
  320.1 27.5 %collective-permute-done.1 = bf16[1,512,768]{2,1,0:T(8,128)(2,1)} collective-permute-done((bf16[1,512,768]{2,1,0:T(8,128)(2,1)}, bf16[1,512,768]{2,1,0:T(8,128)(2,1)}, u32[]{:S(2)}, u32[]{:S(2)}) %collective-permute-start.1) | collective-permute-done | bytes 786464 | tf_op jit(solution)/shard_map/ppermute | solution.py:30
  347.5 1.3 pad_maximum_fusion.1
  349.1 18.4 %fusion.5 = (f32[1024,1536]{1,0:T(8,128)}, f32[1024,1536]{1,0:T(8,128)}) fusion(bf16[1024,768]{1,0:T(8,128)(2,1)S(1)} %bitcast.169, bf16[2,768,1536]{2,1,0:T(8,128)(2,1)} %all-gather.11.cloned.1.call-done), kind=kOutput, calls=%fused_computation.19 | convolution fusion | flops 2513436672 | bytes 16515072 | tf_op jit(solution)/shard_map/dot_general | solution.py:52
  367.5 13.0 %fusion.49 = bf16[1024,768]{1,0:T(8,128)(2,1)} fusion(bf16[2,768,1536]{2,1,0:T(8,128)(2,1)} %all-gather.11.cloned.1.call-done, f32[1024,1536]{1,0:T(8,128)} %get-tuple-element.160, f32[1024,1536]{1,0:T(8,128)} %get-tuple-element.161, bf16[1024,768]{1,0:T(8,128)(2,1)} %all-gather.15.cloned.1.call-done, bf16[2,1536,768]{1,2,0:T(8,128)(2,1)} %all-gather.13.cloned.1.call-done), kind=kOutput, calls=%fused_computation.95 | convolution fusion | flops 4854644736 | bytes 20447232 | tf_op jit(solution)/shard_map/tf,df->td/dot_general | solution.py:64
  380.5 9.1 %fusion.50 = bf16[1024,768]{1,0:T(8,128)(2,1)} fusion(bf16[2,1536,768]{1,2,0:T(8,128)(2,1)} %all-gather.13.cloned.1.call-done, f32[1024,1536]{1,0:T(8,128)} %get-tuple-element.160, f32[1024,1536]{1,0:T(8,128)} %get-tuple-element.161), kind=kOutput, calls=%fused_computation.96 | convolution fusion | flops 2421424128 | bytes 16515072 | tf_op jit(solution)/shard_map/dot_general | solution.py:60
  390.1 16.6 %reduce-scatter.9.cloned.1.call-done = bf16[512,768]{1,0:T(8,128)(2,1)} async-done(((bf16[1024,768]{1,0:T(8,128)(2,1)}), bf16[512,768]{1,0:T(8,128)(2,1)}) %reduce-scatter.9.cloned.1.call-update) | async-done | bytes 786448 | tf_op jit(solution)/shard_map/reduce_scatter | solution.py:229
  406.7 1.5 multiply_reduce_fusion.5
  408.3 26.8 %reduce-scatter.7.cloned.1.call-done = bf16[512,768]{1,0:T(8,128)(2,1)} async-done(((bf16[1024,768]{1,0:T(8,128)(2,1)}), bf16[512,768]{1,0:T(8,128)(2,1)}) %reduce-scatter.7.cloned.1.call-update) | async-done | bytes 786448 | tf_op jit(solution)/shard_map/reduce_scatter | solution.py:206
  435.0 3.1 fusion.101
  438.1 1.1 copy-done.19
  440.5 7.3 fusion.52
  447.8 9.6 %multiply_reduce_fusion.1 = (f32[12,512]{1,0:T(8,128)S(1)}, f32[12,512,512]{1,2,0:T(8,128)}) fusion(f32[12,512]{1,0:T(8,128)S(1)} %log_add_fusion.1, f32[12,512,512]{1,2,0:T(8,128)} %copy-done.1, pred[512,512]{0,1:T(8,128)(4,1)S(1)} %broadcast_compare_fusion, bf16[512,12,64]{0,2,1:T(8,128)(2,1)S(1)} %bitcast.163, bf16[512,12,64]{0,2,1:T(8,128)(2,1)S(1)} %bitcast.161), kind=kOutput, calls=%fused_computation.4 | convolution fusion | flops 418375680 | bytes 27049984 | tf_op jit(solution)/shard_map/while/body/eval_jaxpr/qhd,khd->hqk/dot_general | solution.py:114
  457.4 7.1 multiply_convert_fusion.1
  464.5 2.0 multiply_convert_fusion.12
  466.6 1.1 multiply_convert_fusion.13
  469.1 2.3 multiply_reduce_fusion.4
  472.9 1.3 select_convert_fusion
  474.6 27.1 %all-gather.17.cloned.1.call-done = bf16[1024,768]{1,0:T(8,128)(2,1)} async-done(((bf16[512,768]{1,0:T(8,128)(2,1)}), bf16[1024,768]{1,0:T(8,128)(2,1)}) %all-gather.17.cloned.1.call-update) | async-done | bytes 1572880 | tf_op jit(solution)/shard_map/all_gather | solution.py:225
  501.7 13.0 %fusion.48 = bf16[1024,768]{1,0:T(8,128)(2,1)} fusion(bf16[2,768,1536]{2,1,0:T(8,128)(2,1)} %all-gather.11.cloned.1.call-done, f32[1024,1536]{1,0:T(8,128)} %get-tuple-element.152, f32[1024,1536]{1,0:T(8,128)} %get-tuple-element.153, bf16[1024,768]{1,0:T(8,128)(2,1)} %all-gather.17.cloned.1.call-done, bf16[2,1536,768]{1,2,0:T(8,128)(2,1)} %all-gather.13.cloned.1.call-done), kind=kOutput, calls=%fused_computation.94 | convolution fusion | flops 4854644736 | bytes 20447232 | tf_op jit(solution)/shard_map/tf,df->td/dot_general | solution.py:64
  514.8 1.4 convolution_bitcast_fusion
  516.2 24.7 %reduce-scatter.11.cloned.1.call-done = bf16[512,768]{1,0:T(8,128)(2,1)} async-done(((bf16[1024,768]{1,0:T(8,128)(2,1)}), bf16[512,768]{1,0:T(8,128)(2,1)}) %reduce-scatter.11.cloned.1.call-update) | async-done | bytes 786448 | tf_op jit(solution)/shard_map/reduce_scatter | solution.py:229
  540.9 1.7 multiply_reduce_fusion.3
  542.6 1.8 fusion.97
  546.2 7.5 fusion.55
  553.8 9.5 %multiply_reduce_fusion = (f32[12,512]{1,0:T(8,128)S(1)}, f32[12,512,512]{1,2,0:T(8,128)}) fusion(f32[12,512]{1,0:T(8,128)S(1)} %log_add_fusion, f32[12,512,512]{1,2,0:T(8,128)} %copy-done, pred[512,512]{0,1:T(8,128)(4,1)S(1)} %broadcast_compare_fusion, bf16[512,12,64]{0,2,1:T(8,128)(2,1)S(1)} %bitcast.165, bf16[512,12,64]{0,2,1:T(8,128)(2,1)S(1)} %bitcast.159), kind=kOutput, calls=%fused_computation.1 | convolution fusion | flops 418375680 | bytes 27049984 | tf_op jit(solution)/shard_map/while/body/eval_jaxpr/qhd,khd->hqk/dot_general | solution.py:114
  563.3 7.1 multiply_convert_fusion
  570.4 2.0 multiply_convert_fusion.10
  572.5 1.1 multiply_convert_fusion.11
  574.9 2.2 multiply_reduce_fusion.2
  577.9 1.1 copy-done.7
  579.0 0.9 convolution_bitcast_fusion.1
  585.9 120.7 %all-reduce.7.cloned.1.call-done = f32[76800]{0:T(1024)} async-done(((f32[76800]{0:T(1024)}), f32[76800]{0:T(1024)}) %all-reduce.7.cloned.1.call-update) | async-done | bytes 307216
  706.6 1.4 multiply_reduce_fusion.10
  708.0 2.8 broadcast_select_fusion
  710.8 41.4 %psum.7 = f32[]{:T(128)} all-reduce(f32[]{:T(128)} %multiply_reduce_fusion.10), channel_id=1, replica_groups=mesh['seq'=16,'mlp'=2] {'seq','mlp'}, use_global_device_ids=true, to_apply=%region_28.29 | all-reduce | flops 1 | bytes 8 | tf_op jit(solution)/shard_map/psum | solution.py:260
  752.9 2.7 multiply_subtract_fusion
  (219 shorter events, 20.6 us)
Async XLA Ops:
  8.0 182.6 %all-reduce.5.cloned.1.call-start = ((), (), s32[]{:S(2)}) async-start(), calls=%async_computation.14 | async-start | bytes 614400
  9.8 185.1 %all-gather.7.cloned.1.call-start = ((), (), s32[]{:S(2)}) async-start(), calls=%async_computation.4 | async-start | bytes 7520256 | tf_op jit(solution)/shard_map/all_gather | solution.py:173
  10.3 207.2 %all-gather.9.cloned.1.call-start = ((), (), s32[]{:S(2)}) async-start(), calls=%async_computation.5 | async-start | bytes 2506752 | tf_op jit(solution)/shard_map/all_gather | solution.py:174
  10.9 228.4 %all-gather.11.cloned.1.call-start = ((), (), s32[]{:S(2)}) async-start(), calls=%async_computation.6 | async-start | bytes 5013504 | tf_op jit(solution)/shard_map/all_gather | solution.py:175
  11.5 246.3 %all-gather.13.cloned.1.call-start = ((), (), s32[]{:S(2)}) async-start(), calls=%async_computation.7 | async-start | bytes 5013504 | tf_op jit(solution)/shard_map/all_gather | solution.py:176
  12.2 281.6 %reduce-scatter.5.cloned.1.call-start = ((), (), s32[]{:S(2)}) async-start(), calls=%async_computation.8 | async-start | bytes 2359296 | tf_op jit(solution)/shard_map/reduce_scatter | solution.py:206
  13.8 185.3 %copy-start.52 = (f32[768]{0:T(1024)}, f32[768]{0:T(1024)S(1)}, u32[]{:S(2)}) copy-start(f32[768]{0:T(1024)S(1)} %get-tuple-element.89) | copy-start | bytes 9220
  13.8 208.3 %copy-start.36 = (f32[768]{0:T(1024)}, f32[768]{0:T(1024)S(1)}, u32[]{:S(2)}) copy-start(f32[768]{0:T(1024)S(1)} %get-tuple-element.88) | copy-start | bytes 9220
  194.4 23.1 %copy-start.5 = (f32[512,768]{1,0:T(8,128)}, f32[512,768]{1,0:T(8,128)S(1)}, u32[]{:S(2)}) copy-start(f32[512,768]{1,0:T(8,128)S(1)} %get-tuple-element.136) | copy-start | bytes 4718596
  194.4 4.7 copy-start.46
  194.7 4.4 copy-start.48
  194.8 4.4 copy-start.56
  200.7 3.8 copy-start.10
  204.5 4.7 copy-start
  204.5 5.0 copy-start.34
  204.6 4.7 copy-start.25
  209.2 8.3 %copy-start.38 = (f32[12,512]{1,0:T(8,128)}, f32[12,512]{1,0:T(8,128)S(1)}, u32[]{:S(2)}) copy-start(f32[12,512]{1,0:T(8,128)S(1)} %fusion) | copy-start | bytes 73732
  209.5 8.0 %copy-start.21 = (bf16[512,768]{0,1:T(8,128)(2,1)}, bf16[512,768]{0,1:T(8,128)(2,1)S(1)}, u32[]{:S(2)}) copy-start(bf16[512,768]{0,1:T(8,128)(2,1)S(1)} %copy.60) | copy-start | bytes 2359300
  219.9 19.0 %copy-start.40 = (f32[512]{0:T(512)}, f32[512]{0:T(512)S(1)}, u32[]{:S(2)}) copy-start(f32[512]{0:T(512)S(1)} %broadcast_multiply_fusion.2) | copy-start | bytes 6148
  220.2 19.1 %copy-start.50 = (f32[512]{0:T(512)}, f32[512]{0:T(512)S(1)}, u32[]{:S(2)}) copy-start(f32[512]{0:T(512)S(1)} %multiply_reduce_fusion.8) | copy-start | bytes 6148
  220.3 19.0 %copy-start.42 = (f32[512]{0:T(512)}, f32[512]{0:T(512)S(1)}, u32[]{:S(2)}) copy-start(f32[512]{0:T(512)S(1)} %fusion.76) | copy-start | bytes 6148
  220.5 18.3 %collective-permute-start = (bf16[1,512,768]{2,1,0:T(8,128)(2,1)S(1)}, bf16[1,512,768]{2,1,0:T(8,128)(2,1)S(1)}, u32[]{:S(2)}, u32[]{:S(2)}) collective-permute-start(bf16[1,512,768]{2,1,0:T(8,128)(2,1)S(1)} %fusion.142), channel_id=1, source_target_pairs={{0,1},{1,0},{2,3},{3,2},{4,5},{5,4},{6,7},{7,6},{8,9},{9,8},{10,11... | collective-permute-start | bytes 2359304 | tf_op jit(solution)/shard_map/ppermute | solution.py:30
  257.8 9.4 %copy-start.33 = (f32[38400]{0:T(1024)S(1)}, f32[38400]{0:T(1024)}, u32[]{:S(2)}) copy-start(f32[38400]{0:T(1024)} %get-tuple-element.131) | copy-start | bytes 460804
  257.8 36.1 %copy-start.44 = (s32[512]{0:T(512)S(1)}, s32[512]{0:T(512)}, u32[]{:S(2)}) copy-start(s32[512]{0:T(512)} %param.16) | copy-start | bytes 6148
  266.9 100.6 %all-gather.15.cloned.1.call-start = ((), (), s32[]{:S(2)}) async-start(), calls=%async_computation.10 | async-start | bytes 2359296 | tf_op jit(solution)/shard_map/all_gather | solution.py:225
  296.0 4.7 copy-start.2
  302.3 6.4 copy-start.12
  304.0 4.7 copy-start.16
  308.7 4.5 copy-start.1
  308.7 4.5 copy-start.23
  313.2 3.6 copy-start.3
  313.2 3.6 copy-start.28
  319.2 28.3 %collective-permute-start.1 = (bf16[1,512,768]{2,1,0:T(8,128)(2,1)}, bf16[1,512,768]{2,1,0:T(8,128)(2,1)}, u32[]{:S(2)}, u32[]{:S(2)}) collective-permute-start(bf16[1,512,768]{2,1,0:T(8,128)(2,1)} %fusion.140), channel_id=1, source_target_pairs={{0,1},{1,0},{2,3},{3,2},{4,5},{5,4},{6,7},{7,6},{8,9},{9,8},{10,11... | collective-permute-start | bytes 2359304 | tf_op jit(solution)/shard_map/ppermute | solution.py:30
  319.5 87.2 %reduce-scatter.9.cloned.1.call-start = ((), (), s32[]{:S(2)}) async-start(), calls=%async_computation.11 | async-start | bytes 2359296 | tf_op jit(solution)/shard_map/reduce_scatter | solution.py:229
  380.5 54.6 %reduce-scatter.7.cloned.1.call-start = ((), (), s32[]{:S(2)}) async-start(), calls=%async_computation.9 | async-start | bytes 2359296 | tf_op jit(solution)/shard_map/reduce_scatter | solution.py:206
  389.6 112.0 %all-gather.17.cloned.1.call-start = ((), (), s32[]{:S(2)}) async-start(), calls=%async_computation.12 | async-start | bytes 2359296 | tf_op jit(solution)/shard_map/all_gather | solution.py:225
  435.0 4.2 copy-start.26
  435.0 4.2 copy-start.29
  440.4 7.4 copy-start.24
  440.4 17.0 %slice-start.3 = ((s8[12582912]{0:T(1024)(128)(4,1)}), s8[4194304]{0:T(1024)(128)(4,1)S(1)}, s32[]{:S(2)}) async-start(s8[12582912]{0:T(1024)(128)(4,1)} %bitcast.148), calls=%async_computation.19 | async-start | bytes 8388608
  440.4 17.0 %slice-start.4 = ((s8[12582912]{0:T(1024)(128)(4,1)}), s8[4194304]{0:T(1024)(128)(4,1)S(1)}, s32[]{:S(2)}) async-start(s8[12582912]{0:T(1024)(128)(4,1)} %bitcast.148), calls=%async_computation.20 | async-start | bytes 8388608
  447.8 9.6 %slice-start.5 = ((s8[12582912]{0:T(1024)(128)(4,1)}), s8[4194304]{0:T(1024)(128)(4,1)S(1)}, s32[]{:S(2)}) async-start(s8[12582912]{0:T(1024)(128)(4,1)} %bitcast.148), calls=%async_computation.21 | async-start | bytes 8388608
  457.4 7.1 copy-start.17
  474.3 40.5 %copy-start.8 = (f32[512,768]{1,0:T(8,128)}, f32[512,768]{1,0:T(8,128)S(1)}, u32[]{:S(2)}) copy-start(f32[512,768]{1,0:T(8,128)S(1)} %get-tuple-element.108) | copy-start | bytes 4718596
  474.3 40.4 %copy-start.35 = (f32[12,512]{1,0:T(8,128)S(1)}, f32[12,512]{1,0:T(8,128)}, u32[]{:S(2)}) copy-start(f32[12,512]{1,0:T(8,128)} %copy-done.34) | copy-start | bytes 73732
  474.3 40.4 %copy-start.39 = (f32[12,512]{1,0:T(8,128)S(1)}, f32[12,512]{1,0:T(8,128)}, u32[]{:S(2)}) copy-start(f32[12,512]{1,0:T(8,128)} %copy-done.38) | copy-start | bytes 73732
  474.3 66.6 %copy-start.37 = (f32[768]{0:T(1024)S(1)}, f32[768]{0:T(1024)}, u32[]{:S(2)}) copy-start(f32[768]{0:T(1024)} %copy-done.36) | copy-start | bytes 9220
  474.3 66.6 %copy-start.41 = (f32[512]{0:T(512)S(1)}, f32[512]{0:T(512)}, u32[]{:S(2)}) copy-start(f32[512]{0:T(512)} %copy-done.40) | copy-start | bytes 6148
  474.3 66.6 %reduce-scatter.11.cloned.1.call-start = ((), (), s32[]{:S(2)}) async-start(), calls=%async_computation.13 | async-start | bytes 2359296 | tf_op jit(solution)/shard_map/reduce_scatter | solution.py:229
  514.6 28.0 %copy-start.51 = (f32[512]{0:T(512)S(1)}, f32[512]{0:T(512)}, u32[]{:S(2)}) copy-start(f32[512]{0:T(512)} %copy-done.50) | copy-start | bytes 6148
  514.6 28.0 %copy-start.43 = (f32[512]{0:T(512)S(1)}, f32[512]{0:T(512)}, u32[]{:S(2)}) copy-start(f32[512]{0:T(512)} %copy-done.42) | copy-start | bytes 6148
  514.7 191.9 %all-reduce.7.cloned.1.call-start = ((), (), s32[]{:S(2)}) async-start(), calls=%async_computation.15 | async-start | bytes 614400
  540.9 3.5 copy-start.9
  540.9 3.5 copy-start.18
  540.9 4.1 copy-start.30
  546.2 7.6 copy-start.22
  546.2 17.1 %slice-start = ((s8[12582912]{0:T(1024)(128)(4,1)}), s8[4194304]{0:T(1024)(128)(4,1)S(1)}, s32[]{:S(2)}) async-start(s8[12582912]{0:T(1024)(128)(4,1)} %bitcast.146), calls=%async_computation.16 | async-start | bytes 8388608
  546.2 17.1 %slice-start.1 = ((s8[12582912]{0:T(1024)(128)(4,1)}), s8[4194304]{0:T(1024)(128)(4,1)S(1)}, s32[]{:S(2)}) async-start(s8[12582912]{0:T(1024)(128)(4,1)} %bitcast.146), calls=%async_computation.17 | async-start | bytes 8388608
  553.8 9.5 %slice-start.2 = ((s8[12582912]{0:T(1024)(128)(4,1)}), s8[4194304]{0:T(1024)(128)(4,1)S(1)}, s32[]{:S(2)}) async-start(s8[12582912]{0:T(1024)(128)(4,1)} %bitcast.146), calls=%async_computation.18 | async-start | bytes 8388608
  563.3 7.1 copy-start.15
  577.2 3.6 copy-start.58
  579.0 173.9 %copy-start.45 = (f32[2400]{0:T(1024)S(1)}, f32[2400]{0:T(1024)}, u32[]{:S(2)}) copy-start(f32[2400]{0:T(1024)} %param.23) | copy-start | bytes 28804
  579.0 173.9 %copy-start.54 = (f32[2400]{0:T(1024)S(1)}, f32[2400]{0:T(1024)}, u32[]{:S(2)}) copy-start(f32[2400]{0:T(1024)} %param.25) | copy-start | bytes 28804
  579.0 173.9 %copy-start.55 = (f32[2400]{0:T(1024)S(1)}, f32[2400]{0:T(1024)}, u32[]{:S(2)}) copy-start(f32[2400]{0:T(1024)} %param.24) | copy-start | bytes 28804
  (21 other events, 41.6 us)
Sparse Core Ops, SparseCore 0:
  14.8 175.8 all-reduce.4
  267.0 26.7 reduce-scatter.4
  319.6 36.0 all-gather.14
  380.6 26.1 reduce-scatter.8
  408.9 26.0 reduce-scatter.6
  474.4 27.1 all-gather.16
  514.8 26.0 reduce-scatter.10
  580.9 125.6 all-reduce.6
Sparse Core Ops, SparseCore 1:
  12.8 69.7 all-gather.6
  84.9 41.2 all-gather.8
  128.6 52.4 all-gather.10
  183.7 51.6 all-gather.12
